TPU v7x, 512 devices: a whole 4x8x8 slice. The times are simulated.
512 devices in a mesh: row: 64 (over y, x, core), col: 8 (over z).
Axes of the slice: x: 4, y: 8, z: 8, core: 2. Of those that a mesh axis runs over, the one named last changes fastest.
Arguments:
- hamiltonian: float32 [24576, 24576], P('row', 'col'), as said below
- previous: float32 [24576, 56], P('row', 'col'), may hold values from -6 to 6
- correlation_map: int32 [24576], P('row'), may hold values from 0 to 24575, each once
- lower_cut: float32 [1], replicated, may hold values from 0.5 to 1.5
- upper_bound: float32 [1], replicated, may hold values from 5.5 to 6.5
Outputs:
- basis_out: float32 [24576, 56], P('row', 'col')
- ritz_matrix: float32 [56, 56], replicated
Inputs may be any that keep to these rules, and one draw needn't show every extreme that they name: correlation_map names every index of 0 .. 24575 exactly once. hamiltonian is symmetric.
All inputs are finite; a program needn't handle non-finite values.
Results may differ from a plain program's by a relative error of at most 0.00013.
Values sent between devices are 32-bit elements; how exact they have to be, the bound alone decides.
A program may use at most 64 MiB of HBM per device.

v0:
```python
import jax
import jax.numpy as jnp
from jax import lax
from jax.sharding import PartitionSpec as P

N = 24576
DEG = 4


def body(hamiltonian, previous, correlation_map, lower_cut, upper_bound):
    column_groups = lax.axis_size("col")
    group_width = previous.shape[1]
    width = group_width * column_groups
    centre = (upper_bound[0] + lower_cut[0]) * 0.5
    half_width = (upper_bound[0] - lower_cut[0]) * 0.5
    spread = lax.all_gather(previous, "row", axis=0, tiled=True)
    start_block = jnp.take(spread, correlation_map, axis=0)

    def operate_on(vectors):
        spread_rows = lax.all_gather(vectors, "row", axis=0, tiled=True)
        wanted = lax.all_to_all(spread_rows, "col", split_axis=0, concat_axis=1, tiled=True)
        partial_sum = jnp.dot(hamiltonian, wanted, precision=lax.Precision.HIGHEST)
        return lax.psum_scatter(partial_sum, "col", scatter_dimension=1, tiled=True)

    earlier = start_block
    current = (operate_on(earlier) - centre * earlier) / half_width
    for repeat in range(DEG - 1):
        following = 2.0 * (operate_on(current) - centre * current) / half_width - earlier
        earlier = current
        current = following
    column_index = lax.axis_index("col")
    full_rows = lax.all_gather(current, "col", axis=1, tiled=True)
    empty = jnp.zeros((width, width), jnp.float32)
    block_rows = jnp.dot(current.T, full_rows, precision=lax.Precision.HIGHEST)
    gram_part = lax.dynamic_update_slice_in_dim(empty, block_rows, column_index * group_width, 0)
    gram_total = lax.psum(gram_part, ("row", "col"))
    applied = operate_on(current)
    block_cols = jnp.dot(full_rows.T, applied, precision=lax.Precision.HIGHEST)
    proj_total = lax.psum(
        lax.dynamic_update_slice_in_dim(empty, block_cols, column_index * group_width, 1),
        ("row", "col"),
    )
    gram_matrix = gram_total / N
    projected = proj_total / N
    factor = jnp.linalg.cholesky(gram_matrix)
    identity = jnp.eye(width, dtype=jnp.float32)
    inverse = lax.linalg.triangular_solve(factor, identity, left_side=True, lower=True)
    own_columns = lax.dynamic_slice_in_dim(inverse.T, column_index * group_width, group_width, 1)
    basis_out = jnp.dot(full_rows, own_columns, precision=lax.Precision.HIGHEST)
    ritz_matrix = jnp.dot(
        jnp.dot(inverse, projected, precision=lax.Precision.HIGHEST),
        inverse.T,
        precision=lax.Precision.HIGHEST,
    )
    return (basis_out, ritz_matrix)


def solution(mesh):
    return jax.shard_map(
        body,
        mesh=mesh,
        in_specs=(P("row", "col"), P("row", "col"), P("row"), P(), P()),
        out_specs=(P("row", "col"), P()),
        check_vma=False,
    )
```

profile of v0, /device:TPU:1, one launch (start us, length us, event | category | flops | bytes accessed | tf_op | source)
XLA Modules:
  0.0 1014.7 jit_solution(17210025577529272954)
XLA Ops:
  7.2 0.7 compare_select_fusion
  7.9 0.7 compare_and_fusion
  8.6 0.8 copy.41
  9.4 70.1 %all_gather.21 = f32[24576,7]{1,0:T(8,128)} all-gather(f32[384,7]{1,0:T(8,128)S(1)} %copy.41), channel_id=1, replica_groups=mesh['row'=64,'col'=8] {'row'}, dimensions={0}, use_global_device_ids=true | all-gather | bytes 698880 | tf_op jit(solution)/shard_map/all_gather | solution.py:16
  79.6 5.7 gather_fusion
  85.4 48.9 %all_gather.22 = f32[24576,7]{0,1:T(8,128)S(1)} all-gather(f32[384,7]{0,1:T(8,128)S(1)} %broadcast_select_fusion), channel_id=1, replica_groups=mesh['row'=64,'col'=8] {'row'}, dimensions={0}, use_global_device_ids=true | all-gather | bytes 698880 | tf_op jit(solution)/shard_map/all_gather | solution.py:20
  134.3 30.6 %all_to_all.95 = f32[8,3072,7]{1,2,0:T(8,128)S(1)} all-to-all(f32[8,3072,7]{1,2,0:T(8,128)S(1)} %bitcast.63), channel_id=1, replica_groups=mesh['row'=64,'col'=8] {'col'}, dimensions={0} | all-to-all | bytes 1376256 | tf_op jit(solution)/shard_map/all_to_all | solution.py:21
  164.8 0.1 all_to_all.73
  164.9 7.4 convolution_bitcast_fusion.4
  173.7 1.3 dynamic-slice.4
  175.7 61.5 %all-reduce.12.cloned.1.call-done = f32[384,56]{0,1:T(8,128)} async-done(((f32[384,56]{0,1:T(8,128)}), f32[384,56]{0,1:T(8,128)}) %all-reduce.12.cloned.1.call-update) | async-done | bytes 86032
  237.2 0.7 fusion.18
  237.9 56.2 %all_gather.23 = f32[24576,7]{0,1:T(8,128)S(1)} all-gather(f32[384,7]{0,1:T(8,128)S(1)} %fusion.18), channel_id=1, replica_groups=mesh['row'=64,'col'=8] {'row'}, dimensions={0}, use_global_device_ids=true | all-gather | bytes 698880 | tf_op jit(solution)/shard_map/all_gather | solution.py:20
  294.1 28.4 %all_to_all.96 = f32[8,3072,7]{1,2,0:T(8,128)S(1)} all-to-all(f32[8,3072,7]{1,2,0:T(8,128)S(1)} %bitcast.68), channel_id=1, replica_groups=mesh['row'=64,'col'=8] {'col'}, dimensions={0} | all-to-all | bytes 1376256 | tf_op jit(solution)/shard_map/all_to_all | solution.py:21
  322.5 0.1 all_to_all.77
  322.6 7.4 convolution_bitcast_fusion.3
  330.1 64.8 %all-reduce.14.cloned.1.call-done = f32[384,56]{0,1:T(8,128)} async-done(((f32[384,56]{0,1:T(8,128)}), f32[384,56]{0,1:T(8,128)}) %all-reduce.14.cloned.1.call-update) | async-done | bytes 86032
  394.9 0.7 fusion.17
  395.6 55.7 %all_gather.24 = f32[24576,7]{0,1:T(8,128)S(1)} all-gather(f32[384,7]{0,1:T(8,128)S(1)} %fusion.17), channel_id=1, replica_groups=mesh['row'=64,'col'=8] {'row'}, dimensions={0}, use_global_device_ids=true | all-gather | bytes 698880 | tf_op jit(solution)/shard_map/all_gather | solution.py:20
  451.4 28.6 %all_to_all.97 = f32[8,3072,7]{1,2,0:T(8,128)S(1)} all-to-all(f32[8,3072,7]{1,2,0:T(8,128)S(1)} %bitcast.69), channel_id=1, replica_groups=mesh['row'=64,'col'=8] {'col'}, dimensions={0} | all-to-all | bytes 1376256 | tf_op jit(solution)/shard_map/all_to_all | solution.py:21
  479.9 0.1 all_to_all.81
  480.0 7.5 convolution_bitcast_fusion.2
  487.5 64.9 %all-reduce.16.cloned.1.call-done = f32[384,56]{0,1:T(8,128)} async-done(((f32[384,56]{0,1:T(8,128)}), f32[384,56]{0,1:T(8,128)}) %all-reduce.16.cloned.1.call-update) | async-done | bytes 86032
  552.4 0.7 fusion.14
  553.2 55.7 %all_gather.25 = f32[24576,7]{0,1:T(8,128)S(1)} all-gather(f32[384,7]{0,1:T(8,128)S(1)} %fusion.14), channel_id=1, replica_groups=mesh['row'=64,'col'=8] {'row'}, dimensions={0}, use_global_device_ids=true | all-gather | bytes 698880 | tf_op jit(solution)/shard_map/all_gather | solution.py:20
  608.8 28.4 %all_to_all.98 = f32[8,3072,7]{1,2,0:T(8,128)S(1)} all-to-all(f32[8,3072,7]{1,2,0:T(8,128)S(1)} %bitcast.70), channel_id=1, replica_groups=mesh['row'=64,'col'=8] {'col'}, dimensions={0} | all-to-all | bytes 1376256 | tf_op jit(solution)/shard_map/all_to_all | solution.py:21
  637.3 7.5 convolution_bitcast_fusion.1
  644.8 64.9 %all-reduce.18.cloned.1.call-done = f32[384,56]{0,1:T(8,128)} async-done(((f32[384,56]{0,1:T(8,128)}), f32[384,56]{0,1:T(8,128)}) %all-reduce.18.cloned.1.call-update) | async-done | bytes 86032
  709.7 0.7 fusion.11
  710.4 60.3 %all_gather.27 = f32[24576,7]{0,1:T(8,128)} all-gather(f32[384,7]{0,1:T(8,128)S(1)} %fusion.11), channel_id=1, replica_groups=mesh['row'=64,'col'=8] {'row'}, dimensions={0}, use_global_device_ids=true | all-gather | bytes 698880 | tf_op jit(solution)/shard_map/all_gather | solution.py:20
  770.7 5.1 all-to-all-start.4
  775.8 33.0 %all-gather = f32[8,7,384]{2,1,0:T(8,128)S(1)} all-gather(f32[1,7,384]{2,1,0:T(8,128)S(1)} %bitcast.71), channel_id=1, replica_groups=mesh['row'=64,'col'=8] {'col'}, dimensions={0}, use_global_device_ids=true | all-gather | bytes 96768 | tf_op jit(solution)/shard_map/all_gather | solution.py:32
  808.8 0.1 all_to_all.89
  808.9 7.4 convolution_bitcast_fusion
  816.4 0.2 fusion.24
  816.6 0.1 dynamic_update_slice.6
  816.7 74.4 %all-reduce.20.cloned.1.call-done = f32[384,56]{0,1:T(8,128)} async-done(((f32[384,56]{0,1:T(8,128)}), f32[384,56]{0,1:T(8,128)}) %all-reduce.20.cloned.1.call-update) | async-done | bytes 86032
  891.1 1.0 fusion.7
  892.1 0.3 dynamic_update_slice.7
  892.4 102.7 %all-reduce.5 = (f32[56,56]{1,0:T(8,128)S(1)}, f32[56,56]{1,0:T(8,128)S(1)}) all-reduce(f32[56,56]{1,0:T(8,128)S(1)} %dynamic_update_slice.6, f32[56,56]{1,0:T(8,128)S(1)} %dynamic_update_slice.7), channel_id=1, replica_groups=mesh['row'=64,'col'=8] {'row','col'}, use_global_device_ids=true, to_apply=%region_4.5 | all-reduce | flops 6272 | bytes 50176 | tf_op jit(solution)/shard_map/psum | solution.py:36
  995.2 5.1 cholesky.16
  1000.3 0.6 compare_reduce_fusion
  1001.0 0.7 fusion
  1001.6 4.3 custom-call.6
  1005.9 0.2 fusion.1
  1006.2 0.8 fusion.19
  1006.9 0.2 fusion.4
  1007.1 0.8 fusion.25
  (22 shorter events, 0.6 us)
Async XLA Ops:
  7.2 230.0 %all-reduce.12.cloned.1.call-start = ((), (), s32[]{:S(2)}) async-start(), calls=%async_computation.5 | async-start | bytes 172032
  172.4 222.5 %all-reduce.14.cloned.1.call-start = ((), (), s32[]{:S(2)}) async-start(), calls=%async_computation.6 | async-start | bytes 172032
  330.0 222.4 %all-reduce.16.cloned.1.call-start = ((), (), s32[]{:S(2)}) async-start(), calls=%async_computation.7 | async-start | bytes 172032
  487.5 222.2 %all-reduce.18.cloned.1.call-start = ((), (), s32[]{:S(2)}) async-start(), calls=%async_computation.8 | async-start | bytes 172032
  770.7 38.1 %all-to-all-start.4 = ((f32[8,3072,7]{1,2,0:T(8,128)}), f32[8,3072,7]{1,2,0:T(8,128)S(1)}, u32[]{:S(2)}, u32[]{:S(2)}) async-start(f32[8,3072,7]{1,2,0:T(8,128)} %bitcast.19), calls=%async_computation.4 | async-start | bytes 1572864 | tf_op jit(solution)/shard_map/all_to_all | solution.py:21
  775.8 115.3 %all-reduce.20.cloned.1.call-start = ((), (), s32[]{:S(2)}) async-start(), calls=%async_computation.9 | async-start | bytes 172032
Sparse Core Ops, SparseCore 0:
  172.5 64.5 all-reduce.11
  330.2 64.6 all-reduce.13
  487.6 64.7 all-reduce.15
  644.9 64.7 all-reduce.17
  816.5 74.5 all-reduce.19
where the time goes:
time: 1020 us; the launch traced here: 1010 us
  blocking collectives  598 us (59%)
  waiting for transfers between devices  330 us (32%)
  matrix products  40.4 us (4%)
  between operations  16.1 us (2%)
  other arithmetic  15.1 us (1%)
    unnamed x10, waiting for transfers between devices  330 us
    all_gather x5, blocking collectives, operate_on(): spread_rows = lax.all_gather(vectors, 'row', axis=0, tiled=True)  277 us
    all_to_all x4, blocking collectives, operate_on(): lax.all_to_all(spread_rows, 'col', split_axis=0, concat_axis=1, tiled=True)  116 us
    psum x1, blocking collectives, body(): gram_total = lax.psum(gram_part, ('row', 'col'))  103 us
    all_gather x1, blocking collectives, body(): spread = lax.all_gather(previous, 'row', axis=0, tiled=True)  70.1 us
    dot_general x5, matrix products, operate_on(): partial_sum = jnp.dot(hamiltonian, wanted, precision=lax.Precision.HIGHEST)  37.2 us
    all_gather x1, blocking collectives, body(): full_rows = lax.all_gather(current, 'col', axis=1, tiled=True)  33 us
  transfers between devices with their start and end apart: 6, of which 5 were waited for; matrix products, arithmetic and copies ran while one was open for 0% of the time, Pallas kernels for 0%

commit v1 on v0

--- a/solution.py
+++ b/solution.py
@@ -17,7 +17,9 @@
     start_block = jnp.take(spread, correlation_map, axis=0)
 
     def operate_on(vectors):
-        spread_rows = lax.all_gather(vectors, "row", axis=0, tiled=True)
+        spread_rows = jnp.concatenate(
+            lax.all_to_all(jnp.stack([vectors] * lax.axis_size("row")), "row", 0, 0), axis=0
+        )
         wanted = lax.all_to_all(spread_rows, "col", split_axis=0, concat_axis=1, tiled=True)
         partial_sum = jnp.dot(hamiltonian, wanted, precision=lax.Precision.HIGHEST)
         return lax.psum_scatter(partial_sum, "col", scatter_dimension=1, tiled=True)

time: 1020 us -> 910 us (0.89)
  blocking collectives: 598 us -> 492 us
    all_gather x5 -> x0, blocking collectives: 277 us -> none  [operate_on(): spread_rows = lax.all_gather(vectors, 'row', axis=0, tiled=True)]
    all_to_all x0 -> x5, blocking collectives: none -> 177 us  [operate_on(): lax.all_to_all(jnp.stack([vectors] * lax.axis_size('row')), 'row', 0, 0)]
where the time goes in v1:
time: 910 us; the launch traced here: 909 us
  blocking collectives  492 us (54%)
  waiting for transfers between devices  331 us (36%)
  matrix products  40.4 us (4%)
  between operations  15.9 us (2%)
  other arithmetic  15.1 us (2%)
  local copies, waits for them, and re-layouts  9.22 us (1%)
    unnamed x10, waiting for transfers between devices  331 us
    all_to_all x5, blocking collectives, operate_on(): lax.all_to_all(jnp.stack([vectors] * lax.axis_size('row')), 'row', 0, 0)  177 us
    all_to_all x4, blocking collectives, operate_on(): lax.all_to_all(spread_rows, 'col', split_axis=0, concat_axis=1, tiled=True)  109 us
    psum x1, blocking collectives, body(): gram_total = lax.psum(gram_part, ('row', 'col'))  103 us
    all_gather x1, blocking collectives, body(): spread = lax.all_gather(previous, 'row', axis=0, tiled=True)  70.1 us
    dot_general x5, matrix products, operate_on(): partial_sum = jnp.dot(hamiltonian, wanted, precision=lax.Precision.HIGHEST)  37.2 us
    all_gather x1, blocking collectives, body(): full_rows = lax.all_gather(current, 'col', axis=1, tiled=True)  33 us
  transfers between devices with their start and end apart: 6, of which 5 were waited for; matrix products, arithmetic and copies ran while one was open for 0% of the time, Pallas kernels for 0%

profile of v1, /device:TPU:1, one launch (start us, length us, event | category | flops | bytes accessed | tf_op | source)
XLA Modules:
  0.0 908.5 jit_solution(9299446606013533600)
XLA Ops:
  7.2 0.7 compare_select_fusion
  7.9 0.7 compare_and_fusion
  8.6 0.8 copy.65
  9.4 70.1 %all_gather.6 = f32[24576,7]{1,0:T(8,128)} all-gather(f32[384,7]{1,0:T(8,128)S(1)} %copy.65), channel_id=1, replica_groups=mesh['row'=64,'col'=8] {'row'}, dimensions={0}, use_global_device_ids=true | all-gather | bytes 698880 | tf_op jit(solution)/shard_map/all_gather | solution.py:16
  79.6 5.7 gather_fusion
  85.5 27.3 %all_to_all.120 = f32[64,384,7]{1,2,0:T(8,128)S(1)} all-to-all(f32[64,384,7]{1,2,0:T(8,128)S(1)} %stack.10), channel_id=1, replica_groups=mesh['row'=64,'col'=8] {'row'}, dimensions={0} | all-to-all | bytes 1376256 | tf_op jit(solution)/shard_map/all_to_all | solution.py:21
  112.8 30.8 %all_to_all.121 = f32[8,3072,7]{1,2,0:T(8,128)S(1)} all-to-all(f32[8,3072,7]{1,2,0:T(8,128)S(1)} %bitcast.63), channel_id=1, replica_groups=mesh['row'=64,'col'=8] {'col'}, dimensions={0} | all-to-all | bytes 1376256 | tf_op jit(solution)/shard_map/all_to_all | solution.py:23
  143.6 0.1 all_to_all.89
  143.7 7.4 convolution_bitcast_fusion.4
  152.5 1.3 dynamic-slice.4
  154.4 62.1 %all-reduce.12.cloned.1.call-done = f32[384,56]{0,1:T(8,128)} async-done(((f32[384,56]{0,1:T(8,128)}), f32[384,56]{0,1:T(8,128)}) %all-reduce.12.cloned.1.call-update) | async-done | bytes 86032
  216.5 0.7 fusion.18
  217.3 37.4 %all_to_all.122 = f32[64,384,7]{1,2,0:T(8,128)S(1)} all-to-all(f32[64,384,7]{1,2,0:T(8,128)S(1)} %stack.11), channel_id=1, replica_groups=mesh['row'=64,'col'=8] {'row'}, dimensions={0} | all-to-all | bytes 1376256 | tf_op jit(solution)/shard_map/all_to_all | solution.py:21
  254.7 26.1 %all_to_all.123 = f32[8,3072,7]{1,2,0:T(8,128)S(1)} all-to-all(f32[8,3072,7]{1,2,0:T(8,128)S(1)} %bitcast.65), channel_id=1, replica_groups=mesh['row'=64,'col'=8] {'col'}, dimensions={0} | all-to-all | bytes 1376256 | tf_op jit(solution)/shard_map/all_to_all | solution.py:23
  280.8 0.1 all_to_all.94
  280.9 7.4 convolution_bitcast_fusion.3
  288.4 65.3 %all-reduce.14.cloned.1.call-done = f32[384,56]{0,1:T(8,128)} async-done(((f32[384,56]{0,1:T(8,128)}), f32[384,56]{0,1:T(8,128)}) %all-reduce.14.cloned.1.call-update) | async-done | bytes 86032
  353.7 0.7 fusion.17
  354.5 37.4 %all_to_all.124 = f32[64,384,7]{1,2,0:T(8,128)S(1)} all-to-all(f32[64,384,7]{1,2,0:T(8,128)S(1)} %stack.12), channel_id=1, replica_groups=mesh['row'=64,'col'=8] {'row'}, dimensions={0} | all-to-all | bytes 1376256 | tf_op jit(solution)/shard_map/all_to_all | solution.py:21
  391.9 26.1 %all_to_all.125 = f32[8,3072,7]{1,2,0:T(8,128)S(1)} all-to-all(f32[8,3072,7]{1,2,0:T(8,128)S(1)} %bitcast.67), channel_id=1, replica_groups=mesh['row'=64,'col'=8] {'col'}, dimensions={0} | all-to-all | bytes 1376256 | tf_op jit(solution)/shard_map/all_to_all | solution.py:23
  417.9 0.1 all_to_all.99
  418.0 7.5 convolution_bitcast_fusion.2
  425.6 65.3 %all-reduce.16.cloned.1.call-done = f32[384,56]{0,1:T(8,128)} async-done(((f32[384,56]{0,1:T(8,128)}), f32[384,56]{0,1:T(8,128)}) %all-reduce.16.cloned.1.call-update) | async-done | bytes 86032
  490.9 0.7 fusion.14
  491.7 37.4 %all_to_all.126 = f32[64,384,7]{1,2,0:T(8,128)S(1)} all-to-all(f32[64,384,7]{1,2,0:T(8,128)S(1)} %stack.13), channel_id=1, replica_groups=mesh['row'=64,'col'=8] {'row'}, dimensions={0} | all-to-all | bytes 1376256 | tf_op jit(solution)/shard_map/all_to_all | solution.py:21
  529.1 26.1 %all_to_all.127 = f32[8,3072,7]{1,2,0:T(8,128)S(1)} all-to-all(f32[8,3072,7]{1,2,0:T(8,128)S(1)} %bitcast.69), channel_id=1, replica_groups=mesh['row'=64,'col'=8] {'col'}, dimensions={0} | all-to-all | bytes 1376256 | tf_op jit(solution)/shard_map/all_to_all | solution.py:23
  555.2 7.5 convolution_bitcast_fusion.1
  562.7 65.3 %all-reduce.18.cloned.1.call-done = f32[384,56]{0,1:T(8,128)} async-done(((f32[384,56]{0,1:T(8,128)}), f32[384,56]{0,1:T(8,128)}) %all-reduce.18.cloned.1.call-update) | async-done | bytes 86032
  628.1 0.7 fusion.11
  628.9 37.5 %all_to_all.128 = f32[64,384,7]{1,2,0:T(8,128)} all-to-all(f32[64,384,7]{1,2,0:T(8,128)S(1)} %stack.14), channel_id=1, replica_groups=mesh['row'=64,'col'=8] {'row'}, dimensions={0} | all-to-all | bytes 1376256 | tf_op jit(solution)/shard_map/all_to_all | solution.py:21
  666.3 5.1 all-to-all-start.9
  671.5 33.0 %all-gather = f32[8,7,384]{2,1,0:T(8,128)S(1)} all-gather(f32[1,7,384]{2,1,0:T(8,128)S(1)} %bitcast.71), channel_id=1, replica_groups=mesh['row'=64,'col'=8] {'col'}, dimensions={0}, use_global_device_ids=true | all-gather | bytes 96768 | tf_op jit(solution)/shard_map/all_gather | solution.py:34
  704.6 0.1 all_to_all.109
  704.7 7.4 convolution_bitcast_fusion
  712.1 0.2 fusion.24
  712.3 0.1 dynamic_update_slice.6
  712.4 72.4 %all-reduce.20.cloned.1.call-done = f32[384,56]{0,1:T(8,128)} async-done(((f32[384,56]{0,1:T(8,128)}), f32[384,56]{0,1:T(8,128)}) %all-reduce.20.cloned.1.call-update) | async-done | bytes 86032
  784.9 1.0 fusion.7
  785.9 0.3 dynamic_update_slice.7
  786.2 102.9 %all-reduce.5 = (f32[56,56]{1,0:T(8,128)S(1)}, f32[56,56]{1,0:T(8,128)S(1)}) all-reduce(f32[56,56]{1,0:T(8,128)S(1)} %dynamic_update_slice.6, f32[56,56]{1,0:T(8,128)S(1)} %dynamic_update_slice.7), channel_id=1, replica_groups=mesh['row'=64,'col'=8] {'row','col'}, use_global_device_ids=true, to_apply=%region_4.5 | all-reduce | flops 6272 | bytes 50176 | tf_op jit(solution)/shard_map/psum | solution.py:38
  889.2 5.1 cholesky.16
  894.4 0.6 compare_reduce_fusion
  895.0 0.7 fusion
  895.7 4.3 custom-call.6
  900.0 0.2 fusion.1
  900.2 0.8 fusion.19
  901.0 0.2 fusion.4
  901.2 0.8 fusion.25
  (27 shorter events, 0.9 us)
Async XLA Ops:
  7.2 209.3 %all-reduce.12.cloned.1.call-start = ((), (), s32[]{:S(2)}) async-start(), calls=%async_computation.10 | async-start | bytes 172032
  151.2 202.5 %all-reduce.14.cloned.1.call-start = ((), (), s32[]{:S(2)}) async-start(), calls=%async_computation.11 | async-start | bytes 172032
  288.3 202.6 %all-reduce.16.cloned.1.call-start = ((), (), s32[]{:S(2)}) async-start(), calls=%async_computation.12 | async-start | bytes 172032
  425.5 202.6 %all-reduce.18.cloned.1.call-start = ((), (), s32[]{:S(2)}) async-start(), calls=%async_computation.13 | async-start | bytes 172032
  666.3 38.2 %all-to-all-start.9 = ((f32[8,3072,7]{1,2,0:T(8,128)}), f32[8,3072,7]{1,2,0:T(8,128)S(1)}, u32[]{:S(2)}, u32[]{:S(2)}) async-start(f32[8,3072,7]{1,2,0:T(8,128)} %bitcast.19), calls=%async_computation.9 | async-start | bytes 1572864 | tf_op jit(solution)/shard_map/all_to_all | solution.py:23
  671.4 113.4 %all-reduce.20.cloned.1.call-start = ((), (), s32[]{:S(2)}) async-start(), calls=%async_computation.14 | async-start | bytes 172032
Sparse Core Ops, SparseCore 0:
  151.3 65.1 all-reduce.11
  288.4 65.1 all-reduce.13
  425.6 65.2 all-reduce.15
  562.8 65.1 all-reduce.17
  712.2 72.5 all-reduce.19
